TPU v7x, 32 devices: a whole 2x2x4 slice. The times are simulated.
32 devices in a mesh: groups: 2 (over y), rows: 16 (over z, x, core), cols: 1.
Axes of the slice: x: 2, y: 2, z: 4, core: 2. Of those that a mesh axis runs over, the one named last changes fastest.
Arguments:
- pair_in: bfloat16 [256, 128, 128], P(('groups', 'rows'), 'cols'), parts along dimension 0, may hold values from -6 to 450
- single_in: float32 [256, 384], P(('groups', 'rows')), parts along dimension 0, may hold values from -6 to 6
- frames_in: float32 [12, 256], P(None, ('groups', 'rows')), parts along dimension 1, may hold values from -3 to 3, as said below
- dist_bins: int32 [2, 256, 128], P(None, ('groups', 'rows'), 'cols'), parts along dimension 1, may hold values from 0 to 14
- res_mask: int32 [256], P('groups'), parts along dimension 0, may hold values from 0 to 1, as said below
- chain_ids: int32 [256], P('groups'), parts along dimension 0, may hold values from 0 to 7, never falling along the last dimension, each value on 1 to 32 neighbouring positions
- w_left: bfloat16 [384, 128], replicated, may hold values from -0.3125 to 0.3125
- w_right: bfloat16 [384, 128], replicated, may hold values from -0.3125 to 0.3125
- dist_embed: bfloat16 [15, 128], replicated, may hold values from -6 to 6
- chain_embed: bfloat16 [2, 128], replicated, may hold values from -6 to 6
- pair_gain: float32 [128], replicated, may hold values from 0.5 to 1.5
- mlp_in: bfloat16 [128, 512], replicated, may hold values from -0.5 to 0.5
- mlp_bias: float32 [512], replicated, may hold values from -3 to 3
- mlp_out: bfloat16 [512, 128], replicated, may hold values from -0.25 to 0.25
- w_qkv: bfloat16 [384, 576], replicated, may hold values from -0.3125 to 0.3125
- w_points: bfloat16 [384, 576], replicated, may hold values from -0.3125 to 0.3125
- bias_weight: bfloat16 [128, 12], replicated, may hold values from -0.5 to 0.5
- point_scale: float32 [12], replicated, may hold values from 0.3 to 3
- w_out: bfloat16 [2112, 384], replicated, may hold values from -0.125 to 0.125
- single_gain: float32 [384], replicated, may hold values from 0.5 to 1.5
- w_frame: bfloat16 [384, 6], replicated, may hold values from -0.3125 to 0.3125
Outputs:
- pair_out: bfloat16 [256, 128, 128], P(('groups', 'rows'), 'cols'), parts along dimension 0
- single_out: float32 [256, 384], P(('groups', 'rows')), parts along dimension 0
- frames_out: float32 [12, 256], P(None, ('groups', 'rows')), parts along dimension 1
There are 2 independent parts, one for each index of `groups`. A program takes and returns all parts, laid end to end along the dimension named above; an argument that names none is the same for every part. Nothing has to cross between parts.
Inputs may be any that keep to these rules, and one draw needn't show every extreme that they name: `frames_in`: column n holds a rotation matrix in rows 0 to 8 (row-major) and a translation in rows 9 to 11. `res_mask`: 1 on a prefix of the residues, at least 64 and at most 127 of them. `chain_ids`: never falling along the residues; a chain holds 1 to 32 residues.
All inputs are finite; a program needn't handle non-finite values.
Results may differ from a plain program's by a relative error of at most 0.022.
Values may be sent and summed in bfloat16 or wider, within the bound.
A program may use at most 64 MiB of HBM per device.

v0:
```python
import math

import jax
import jax.numpy as jnp
from jax import lax
from jax.sharding import PartitionSpec as P

NQP = 4
CYCLES = 2


HIGHEST = lax.Precision.HIGHEST


def layer_norm(values, norm_gain):
    centre = jnp.mean(values, axis=-1, keepdims=True)
    spread = values - centre
    second = jnp.mean(spread * spread, axis=-1, keepdims=True)
    return spread * lax.rsqrt(second + 1e-05) * norm_gain


def to_global(points, frames):
    turns = frames[:, :9].reshape(-1, 3, 3)
    return jnp.einsum("nab,nbx->nax", turns, points, precision=HIGHEST) + frames[:, 9:12, None]


def to_local(points, frames):
    turns = frames[:, :9].reshape(-1, 3, 3)
    return jnp.einsum("nab,nax->nbx", turns, points - frames[:, 9:12, None], precision=HIGHEST)


def update_frames(frames, frame_step):
    quat_scale = lax.rsqrt(1.0 + jnp.sum(frame_step[:, :3] * frame_step[:, :3], axis=1))
    quat_b = frame_step[:, 0] * quat_scale
    quat_c = frame_step[:, 1] * quat_scale
    quat_d = frame_step[:, 2] * quat_scale
    entries = [
        quat_scale * quat_scale + quat_b * quat_b - quat_c * quat_c - quat_d * quat_d,
        2.0 * (quat_b * quat_c - quat_scale * quat_d),
        2.0 * (quat_b * quat_d + quat_scale * quat_c),
        2.0 * (quat_b * quat_c + quat_scale * quat_d),
        quat_scale * quat_scale - quat_b * quat_b + quat_c * quat_c - quat_d * quat_d,
        2.0 * (quat_c * quat_d - quat_scale * quat_b),
        2.0 * (quat_b * quat_d - quat_scale * quat_c),
        2.0 * (quat_c * quat_d + quat_scale * quat_b),
        quat_scale * quat_scale - quat_b * quat_b - quat_c * quat_c + quat_d * quat_d,
    ]
    turn_matrix = jnp.stack(entries, axis=1).reshape(-1, 3, 3)
    before = frames[:, :9].reshape(-1, 3, 3)
    rotated = jnp.einsum("nab,nbc->nac", before, turn_matrix, precision=HIGHEST)
    new_shift = (
        jnp.einsum("nab,nb->na", before, frame_step[:, 3:6], precision=HIGHEST) + frames[:, 9:12]
    )
    return jnp.concatenate([rotated.reshape(-1, 9), new_shift], axis=1)


def update_row(
    pair_row,
    bins_row,
    left_row,
    mask_row,
    same_row,
    right_keys,
    dist_embed,
    chain_embed,
    pair_gain,
    mlp_in,
    mlp_bias,
    mlp_out,
):
    onehot = (
        bins_row[:, None] == jnp.arange(dist_embed.shape[0], dtype=jnp.int32)[None, :]
    ).astype(jnp.bfloat16)
    looked = jnp.dot(onehot, dist_embed, preferred_element_type=jnp.float32)
    chain_part = jnp.where(
        same_row[:, None], chain_embed[1].astype(jnp.float32), chain_embed[0].astype(jnp.float32)
    )
    summed = (
        pair_row.astype(jnp.float32)
        + mask_row[:, None] * (left_row[None, :] + right_keys.astype(jnp.float32))
        + looked
        + chain_part
    )
    normed = layer_norm(summed, pair_gain).astype(jnp.bfloat16)
    hidden = jax.nn.relu(
        jnp.dot(normed, mlp_in, preferred_element_type=jnp.float32) + mlp_bias
    ).astype(jnp.bfloat16)
    mixed_out = jnp.dot(hidden, mlp_out, preferred_element_type=jnp.float32)
    return (summed + mask_row[:, None] * mixed_out).astype(jnp.bfloat16)


def attention_logits(
    queries, query_points, key_heads, key_points, pair_tile, key_live, bias_weight, point_scale
):
    head_dim = queries.shape[2]
    scores = jnp.einsum(
        "ihd,jhd->ihj", queries, key_heads, preferred_element_type=jnp.float32
    ) * head_dim ** (-0.5)
    biases = jnp.einsum("ijc,ch->ihj", pair_tile, bias_weight, preferred_element_type=jnp.float32)
    query_sq = jnp.sum(query_points * query_points, axis=(1, 3))
    key_sq = jnp.sum(key_points * key_points, axis=(1, 3))
    cross_term = jnp.einsum("iahp,jahp->ihj", query_points, key_points, precision=HIGHEST)
    distance = query_sq[:, :, None] + key_sq.T[None, :, :] - 2.0 * cross_term
    point_weight = math.sqrt(2.0 / (9.0 * query_points.shape[3])) / 2.0
    logits = math.sqrt(1.0 / 3.0) * (
        scores + biases - point_scale[None, :, None] * point_weight * distance
    )
    return jnp.where(key_live[None, None, :], logits, -1e30)


def build_features(row_total, attended, point_sum, pair_sum, frames_rows):
    row_count = row_total.shape[0]
    attended = attended / row_total[:, :, None]
    point_sum = point_sum / row_total[:, None, :, None]
    pair_sum = pair_sum / row_total[:, :, None]
    local_points = to_local(point_sum.reshape(row_count, 3, -1), frames_rows).reshape(
        point_sum.shape
    )
    lengths = jnp.sqrt(jnp.sum(local_points * local_points, axis=1) + 1.0)
    return jnp.concatenate(
        [
            attended.reshape(row_count, -1),
            local_points.reshape(row_count, -1),
            lengths.reshape(row_count, -1),
            pair_sum.reshape(row_count, -1),
        ],
        axis=1,
    ).astype(jnp.bfloat16)


def finish_rows(
    single_rows,
    frames_rows,
    row_total,
    attended,
    point_sum,
    pair_sum,
    head_count,
    head_dim,
    value_count,
    channels,
    w_out,
    single_gain,
    w_frame,
):
    rows_here = single_rows.shape[0]
    features = build_features(
        row_total,
        attended.reshape(rows_here, head_count, head_dim),
        point_sum.reshape(rows_here, 3, head_count, value_count),
        pair_sum.reshape(rows_here, head_count, channels),
        frames_rows,
    )
    update = jnp.dot(features, w_out, preferred_element_type=jnp.float32)
    single_rows = layer_norm(single_rows + update, single_gain)
    frame_step = jnp.dot(
        single_rows.astype(jnp.bfloat16), w_frame, preferred_element_type=jnp.float32
    )
    return (single_rows, update_frames(frames_rows, frame_step))


def shards(
    pair_in,
    single_in,
    frames_in,
    dist_bins,
    res_mask,
    chain_ids,
    w_left,
    w_right,
    dist_embed,
    chain_embed,
    pair_gain,
    mlp_in,
    mlp_bias,
    mlp_out,
    w_qkv,
    w_points,
    bias_weight,
    point_scale,
    w_out,
    single_gain,
    w_frame,
):
    row_count = pair_in.shape[0]
    key_count = pair_in.shape[1]
    channels = pair_in.shape[2]
    head_count = bias_weight.shape[1]
    head_dim = w_qkv.shape[1] // (3 * head_count)
    point_count = w_points.shape[1] // (3 * head_count)
    value_count = point_count - 2 * NQP
    row_start = lax.axis_index("rows") * row_count
    key_start = lax.axis_index("cols") * key_count
    row_live = lax.dynamic_slice_in_dim(res_mask, row_start, row_count).astype(jnp.float32)
    key_mask_int = lax.dynamic_slice_in_dim(res_mask, key_start, key_count)
    key_live = key_mask_int > 0
    pair_mask = row_live[:, None] * key_mask_int.astype(jnp.float32)[None, :]
    same_chain = (
        lax.dynamic_slice_in_dim(chain_ids, row_start, row_count)[:, None]
        == lax.dynamic_slice_in_dim(chain_ids, key_start, key_count)[None, :]
    )
    pair_tile = pair_in
    single = single_in
    frames = frames_in.T
    for cycle_index in range(CYCLES):
        single_bf = single.astype(jnp.bfloat16)
        left_proj = jnp.dot(single_bf, w_left, preferred_element_type=jnp.float32)
        triple = (
            jnp.dot(single_bf, w_qkv, preferred_element_type=jnp.float32)
            .astype(jnp.bfloat16)
            .reshape(row_count, 3, head_count, head_dim)
        )
        own_points = to_global(
            jnp.dot(single_bf, w_points, preferred_element_type=jnp.float32).reshape(
                row_count, 3, head_count * point_count
            ),
            frames,
        ).reshape(row_count, 3, head_count, point_count)
        own_right = jnp.dot(single_bf, w_right, preferred_element_type=jnp.float32).astype(
            jnp.bfloat16
        )
        own_pairs = triple[:, 1:].reshape(row_count, -1)
        own_geometry = own_points[:, :, :, NQP:].reshape(row_count, -1)
        all_right, all_pairs = (
            lax.all_gather(own_right, "rows", axis=0, tiled=True),
            lax.all_gather(own_pairs, "rows", axis=0, tiled=True),
        )
        all_geometry = lax.all_gather(own_geometry, "rows", axis=0, tiled=True)
        right_keys = lax.dynamic_slice_in_dim(all_right, key_start, key_count)
        key_pairs = lax.dynamic_slice_in_dim(all_pairs, key_start, key_count)
        key_geometry = lax.dynamic_slice_in_dim(all_geometry, key_start, key_count)
        key_geometry = key_geometry.reshape(key_count, 3, head_count, point_count - NQP)
        key_heads = key_pairs.reshape(key_count, 2, head_count, head_dim)

        def row_step(inputs):
            return update_row(
                inputs[0],
                inputs[1],
                inputs[2],
                inputs[3],
                inputs[4],
                right_keys,
                dist_embed,
                chain_embed,
                pair_gain,
                mlp_in,
                mlp_bias,
                mlp_out,
            )

        pair_tile = lax.map(
            row_step, (pair_tile, dist_bins[cycle_index], left_proj, pair_mask, same_chain)
        )
        logits = attention_logits(
            triple[:, 0],
            own_points[:, :, :, :NQP],
            key_heads[:, 0],
            key_geometry[:, :, :, :NQP],
            pair_tile,
            key_live,
            bias_weight,
            point_scale,
        )
        row_top = lax.pmax(jnp.max(logits, axis=2), "cols")
        weights = jnp.where(
            key_live[None, None, :], jnp.exp(logits - row_top[:, :, None]), 0.0
        ).astype(jnp.bfloat16)
        row_total = jnp.sum(weights.astype(jnp.float32), axis=2)
        attended = jnp.einsum(
            "ihj,jhd->ihd", weights, key_heads[:, 1], preferred_element_type=jnp.float32
        )
        point_sum = jnp.einsum(
            "ihj,jahp->iahp",
            weights.astype(jnp.float32),
            key_geometry[:, :, :, NQP:],
            precision=HIGHEST,
        )
        pair_sum = jnp.einsum(
            "ihj,ijc->ihc", weights, pair_tile, preferred_element_type=jnp.float32
        )
        row_total, attended, point_sum, pair_sum = (
            lax.psum(row_total.astype(jnp.bfloat16), "cols").astype(jnp.float32),
            lax.psum(attended.reshape(row_count, -1).astype(jnp.bfloat16), "cols").astype(
                jnp.float32
            ),
            lax.psum(point_sum.reshape(row_count, -1).astype(jnp.bfloat16), "cols").astype(
                jnp.float32
            ),
            lax.psum(pair_sum.reshape(row_count, -1).astype(jnp.bfloat16), "cols").astype(
                jnp.float32
            ),
        )
        single, frames = finish_rows(
            single,
            frames,
            row_total,
            attended,
            point_sum,
            pair_sum,
            head_count,
            head_dim,
            value_count,
            channels,
            w_out,
            single_gain,
            w_frame,
        )
    return (pair_tile, single, frames.T)


def solution(mesh):
    in_specs = (
        P(("groups", "rows"), "cols", None),
        P(("groups", "rows"), None),
        P(None, ("groups", "rows")),
        P(None, ("groups", "rows"), "cols"),
        P("groups"),
        P("groups"),
        P(),
        P(),
        P(),
        P(),
        P(),
        P(),
        P(),
        P(),
        P(),
        P(),
        P(),
        P(),
        P(),
        P(),
        P(),
    )
    out_specs = (
        P(("groups", "rows"), "cols", None),
        P(("groups", "rows"), None),
        P(None, ("groups", "rows")),
    )
    return jax.shard_map(shards, mesh=mesh, in_specs=in_specs, out_specs=out_specs, check_vma=False)
```

profile of v0, /device:TPU:0, one launch (start us, length us, event | category | flops | bytes accessed | tf_op | source)
XLA Modules:
  0.0 194.5 jit_solution(276466925991388244)
XLA Ops:
  0.6 0.8 convert_element_type.191
  2.9 1.0 fusion.123
  4.0 1.0 convolution_convert_fusion.9
  5.0 23.2 %all_gather.18 = bf16[128,128]{1,0:T(8,128)(2,1)S(1)} all-gather(bf16[8,128]{1,0:T(8,128)(2,1)S(1)} %convolution_convert_fusion.9), channel_id=1, replica_groups=mesh['groups'=2,'rows'=16,'cols'=1] {'rows'}, dimensions={0}, use_global_device_ids=true | all-gather | bytes 34816 | tf_op jit(solution)/shard_map/all_gather | solution.py:225
  28.3 1.3 slice_bitcast_fusion.8
  31.1 33.2 %while.20 = (s32[]{:T(128)}, bf16[8,128,128]{1,2,0:T(8,128)(2,1)S(1)}, bf16[8,128,128]{2,1,0:T(8,128)(2,1)}, f32[8,128]{1,0:T(8,128)S(1)}, f32[8,128]{1,0:T(8,12...) while((s32[]{:T(128)}, ...), condition=%wide.region_3.4_spmd, body=%wide.region_0.3_spmd.sunk | while | flops 34556160 | bytes 772905 | solution.py:251
  32.8 1.0 fusion.202
  33.8 1.5 fusion.203
  36.9 1.0 fusion.202
  37.9 1.5 fusion.203
  41.1 1.0 fusion.202
  42.1 1.5 fusion.203
  45.2 1.0 fusion.202
  46.2 1.5 fusion.203
  49.4 1.0 fusion.202
  50.4 1.5 fusion.203
  53.5 1.0 fusion.202
  54.6 1.5 fusion.203
  57.7 1.0 fusion.202
  58.7 1.5 fusion.203
  61.9 1.0 fusion.202
  62.9 1.5 fusion.203
  65.9 18.1 %all_gather.20 = f32[128,432]{1,0:T(8,128)S(1)} all-gather(f32[8,432]{1,0:T(8,128)S(1)} %reshape.270), channel_id=1, replica_groups=mesh['groups'=2,'rows'=16,'cols'=1] {'rows'}, dimensions={0}, use_global_device_ids=true | all-gather | bytes 235008 | tf_op jit(solution)/shard_map/all_gather | solution.py:228
  85.2 19.0 %all_gather.19 = bf16[128,384]{1,0:T(8,128)(2,1)S(1)} all-gather(bf16[8,384]{1,0:T(8,128)(2,1)S(1)} %reshape.265), channel_id=1, replica_groups=mesh['groups'=2,'rows'=16,'cols'=1] {'rows'}, dimensions={0}, use_global_device_ids=true | all-gather | bytes 104448 | tf_op jit(solution)/shard_map/all_gather | solution.py:226
  107.9 0.9 multiply_reduce_fusion.7
  109.6 1.0 fusion.92
  111.4 1.1 fusion.118
  113.1 17.6 %all_gather.21 = bf16[128,128]{1,0:T(8,128)(2,1)S(1)} all-gather(bf16[8,128]{1,0:T(8,128)(2,1)S(1)} %convolution_convert_fusion.8), channel_id=1, replica_groups=mesh['groups'=2,'rows'=16,'cols'=1] {'rows'}, dimensions={0}, use_global_device_ids=true | all-gather | bytes 34816 | tf_op jit(solution)/shard_map/all_gather | solution.py:225
  130.9 17.7 %while.21 = (s32[]{:T(128)}, bf16[8,128,128]{1,2,0:T(8,128)(2,1)S(1)}, bf16[8,128,128]{1,2,0:T(8,128)(2,1)S(1)}, f32[8,128]{1,0:T(8,128)}, f32[8,128]{1,0:T(8,12...) while((s32[]{:T(128)}, ...), condition=%wide.region_14.15_spmd, body=%wide.region_11.14_spmd.sunk | while | flops 34556160 | bytes 641833 | solution.py:251
  148.7 0.9 copy.108
  151.5 19.4 %all_gather.23 = f32[128,432]{1,0:T(8,128)S(1)} all-gather(f32[8,432]{1,0:T(8,128)S(1)} %reshape.281), channel_id=1, replica_groups=mesh['groups'=2,'rows'=16,'cols'=1] {'rows'}, dimensions={0}, use_global_device_ids=true | all-gather | bytes 235008 | tf_op jit(solution)/shard_map/all_gather | solution.py:228
  172.0 17.8 %all_gather.22 = bf16[128,384]{1,0:T(8,128)(2,1)S(1)} all-gather(bf16[8,384]{1,0:T(8,128)(2,1)S(1)} %reshape.276), channel_id=1, replica_groups=mesh['groups'=2,'rows'=16,'cols'=1] {'rows'}, dimensions={0}, use_global_device_ids=true | all-gather | bytes 104448 | tf_op jit(solution)/shard_map/all_gather | solution.py:226
  (331 shorter events, 49.9 us)
Async XLA Ops:
  0.6 110.8 %copy-start = (bf16[2112,384]{1,0:T(8,128)(2,1)S(1)}, bf16[2112,384]{1,0:T(8,128)(2,1)}, u32[]{:S(2)}) copy-start(bf16[2112,384]{1,0:T(8,128)(2,1)} %param.43) | copy-start | bytes 4866052
  31.1 33.3 %copy-start.25 = (s32[128]{0:T(128)S(1)}, s32[128]{0:T(128)}, u32[]{:S(2)}) copy-start(s32[128]{0:T(128)} %param.29) | copy-start | bytes 1540
  31.1 33.3 %copy-start.3 = (bf16[384,576]{0,1:T(8,128)(2,1)S(1)}, bf16[384,576]{0,1:T(8,128)(2,1)}, u32[]{:S(2)}) copy-start(bf16[384,576]{0,1:T(8,128)(2,1)} %param.40) | copy-start | bytes 1327108
  31.1 33.6 %copy-start.19 = (f32[12,8]{0,1:T(8,128)S(1)}, f32[12,8]{0,1:T(8,128)}, u32[]{:S(2)}) copy-start(f32[12,8]{0,1:T(8,128)} %param.27) | copy-start | bytes 1156
  64.3 0.9 copy-start.12
  64.4 0.9 copy-start.22
  64.4 40.2 %copy-start.27 = (pred[128]{0:T(512)(128)(4,1)}, pred[128]{0:T(512)(128)(4,1)S(1)}, u32[]{:S(2)}) copy-start(pred[128]{0:T(512)(128)(4,1)S(1)} %broadcast_compare_fusion.1) | copy-start | bytes 388
  64.6 19.7 %copy-start.26 = (f32[12]{0:T(128)S(1)}, f32[12]{0:T(128)}, u32[]{:S(2)}) copy-start(f32[12]{0:T(128)} %param.42) | copy-start | bytes 148
  64.9 42.0 %copy-start.15 = (f32[8,3]{0,1:T(4,128)}, f32[8,3]{0,1:T(4,128)S(1)}, u32[]{:S(2)}) copy-start(f32[8,3]{0,1:T(4,128)S(1)} %slice.143) | copy-start | bytes 292
  65.3 19.5 %copy-start.4 = (bf16[384,576]{0,1:T(8,128)(2,1)S(1)}, bf16[384,576]{0,1:T(8,128)(2,1)}, u32[]{:S(2)}) copy-start(bf16[384,576]{0,1:T(8,128)(2,1)} %param.39) | copy-start | bytes 1327108
  65.8 38.6 %copy-start.17 = (bf16[128,12]{0,1:T(8,128)(2,1)S(1)}, bf16[128,12]{0,1:T(8,128)(2,1)}, u32[]{:S(2)}) copy-start(bf16[128,12]{0,1:T(8,128)(2,1)} %param.41) | copy-start | bytes 9220
  84.4 0.9 copy-start.20
  104.9 1.8 copy-start.29
  104.9 2.0 %copy-start.16 = (bf16[8,12]{0,1:T(8,128)(2,1)}, bf16[8,12]{0,1:T(8,128)(2,1)S(1)}, u32[]{:S(2)}) copy-start(bf16[8,12]{0,1:T(8,128)(2,1)S(1)} %get-tuple-element.307) | copy-start | bytes 580
  106.7 6.1 %copy-start.13 = (f32[384]{0:T(512)S(1)}, f32[384]{0:T(512)}, u32[]{:S(2)}) copy-start(f32[384]{0:T(512)} %param.44) | copy-start | bytes 4612
  106.7 6.1 %copy-start.5 = (bf16[384,128]{1,0:T(8,128)(2,1)S(1)}, bf16[384,128]{1,0:T(8,128)(2,1)}, u32[]{:S(2)}) copy-start(bf16[384,128]{1,0:T(8,128)(2,1)} %param.31) | copy-start | bytes 294916
  106.7 6.3 %copy-start.6 = (bf16[384,128]{1,0:T(8,128)(2,1)S(1)}, bf16[384,128]{1,0:T(8,128)(2,1)}, u32[]{:S(2)}) copy-start(bf16[384,128]{1,0:T(8,128)(2,1)} %param.32) | copy-start | bytes 294916
  106.9 23.9 %copy-start.1 = (bf16[128,512]{1,0:T(8,128)(2,1)S(1)}, bf16[128,512]{1,0:T(8,128)(2,1)}, u32[]{:S(2)}) copy-start(bf16[128,512]{1,0:T(8,128)(2,1)} %get-tuple-element.600) | copy-start | bytes 393220
  106.9 23.9 %copy-start.2 = (bf16[512,128]{1,0:T(8,128)(2,1)S(1)}, bf16[512,128]{1,0:T(8,128)(2,1)}, u32[]{:S(2)}) copy-start(bf16[512,128]{1,0:T(8,128)(2,1)} %get-tuple-element.601) | copy-start | bytes 393220
  106.9 23.9 %copy-start.7 = (f32[512]{0:T(512)S(1)}, f32[512]{0:T(512)}, u32[]{:S(2)}) copy-start(f32[512]{0:T(512)} %get-tuple-element.602) | copy-start | bytes 6148
  107.0 23.9 %copy-start.8 = (bf16[2,128]{1,0:T(2,128)(2,1)S(1)}, bf16[2,128]{1,0:T(2,128)(2,1)}, u32[]{:S(2)}) copy-start(bf16[2,128]{1,0:T(2,128)(2,1)} %get-tuple-element.603) | copy-start | bytes 1540
  107.0 23.9 %copy-start.9 = (f32[128]{0:T(128)S(1)}, f32[128]{0:T(128)}, u32[]{:S(2)}) copy-start(f32[128]{0:T(128)} %get-tuple-element.604) | copy-start | bytes 1540
  107.1 23.8 %copy-start.23 = (pred[8,128]{1,0:T(8,128)(4,1)S(1)}, pred[8,128]{1,0:T(8,128)(4,1)}, u32[]{:S(2)}) copy-start(pred[8,128]{1,0:T(8,128)(4,1)} %copy-done.22) | copy-start | bytes 3076
  107.1 23.8 %copy-start.24 = (bf16[15,128]{1,0:T(8,128)(2,1)S(1)}, bf16[15,128]{1,0:T(8,128)(2,1)}, u32[]{:S(2)}) copy-start(bf16[15,128]{1,0:T(8,128)(2,1)} %get-tuple-element.607) | copy-start | bytes 11524
  130.9 18.6 %copy-start.11 = (bf16[384,6]{0,1:T(8,128)(2,1)S(1)}, bf16[384,6]{0,1:T(8,128)(2,1)}, u32[]{:S(2)}) copy-start(bf16[384,6]{0,1:T(8,128)(2,1)} %param.45) | copy-start | bytes 13828
  150.3 20.9 %copy-start.21 = (f32[12]{0:T(128)S(1)}, f32[12]{0:T(128)}, u32[]{:S(2)}) copy-start(f32[12]{0:T(128)} %copy-done.20) | copy-start | bytes 148
  151.3 38.7 %copy-start.18 = (bf16[128,12]{0,1:T(8,128)(2,1)S(1)}, bf16[128,12]{0,1:T(8,128)(2,1)}, u32[]{:S(2)}) copy-start(bf16[128,12]{0,1:T(8,128)(2,1)} %param.41) | copy-start | bytes 9220
  151.4 38.7 %copy-start.28 = (pred[128]{0:T(512)(128)(4,1)S(1)}, pred[128]{0:T(512)(128)(4,1)}, u32[]{:S(2)}) copy-start(pred[128]{0:T(512)(128)(4,1)} %copy-done.27) | copy-start | bytes 388
  172.0 20.1 %copy-start.14 = (f32[384]{0:T(512)S(1)}, f32[384]{0:T(512)}, u32[]{:S(2)}) copy-start(f32[384]{0:T(512)} %param.44) | copy-start | bytes 4612
  192.8 1.7 copy-start.10
where the time goes:
time: 197 us; the launch traced here: 195 us
  blocking collectives  115 us (58%)
  matrix products  35.8 us (18%)
  local copies, waits for them, and re-layouts  30 us (15%)
  other arithmetic  11.5 us (6%)
    all_gather x2, blocking collectives, shards(): lax.all_gather(own_right, 'rows', axis=0, tiled=True)  40.7 us
    all_gather x2, blocking collectives, shards(): all_geometry = lax.all_gather(own_geometry, 'rows', axis=0, tiled=True)  37.6 us
    all_gather x2, blocking collectives, shards(): lax.all_gather(own_pairs, 'rows', axis=0, tiled=True)  36.8 us
    dot_general x16, matrix products, update_row(): mixed_out = jnp.dot(hidden, mlp_out, preferred_element_type=jnp.float32)  15.4 us
    dot_general x16, matrix products, update_row(): looked = jnp.dot(onehot, dist_embed, preferred_element_type=jnp.float32)  9.72 us
    dynamic_slice x16, local copies, waits for them, and re-layouts, shards(): lax.map(row_step, (pair_tile, dist_bins[cycle_index], left_proj, pair_mas...  7.02 us
    convert_element_type x16, other arithmetic, update_row(): chain_embed[1].astype(jnp.float32)  5.94 us
    eq x16, local copies, waits for them, and re-layouts, update_row(): bins_row[:, None]  5.66 us

commit v1 on v0

--- a/solution.py
+++ b/solution.py
@@ -1,8 +1,12 @@
+import functools
 import math
 
 import jax
 import jax.numpy as jnp
+import numpy as np
 from jax import lax
+from jax.experimental import pallas as pl
+from jax.experimental.pallas import tpu as pltpu
 from jax.sharding import PartitionSpec as P
 
 NQP = 4
@@ -308,6 +312,440 @@
     return (pair_tile, single, frames.T)
 
 
+BF16 = jnp.bfloat16
+F32 = jnp.float32
+MESH_ID = pl.DeviceIdType.MESH
+
+
+def nn(a, b, precision=None):
+    return lax.dot_general(
+        a, b, (((1,), (0,)), ((), ())), precision=precision, preferred_element_type=F32
+    )
+
+
+def nt(a, b, precision=None):
+    return lax.dot_general(
+        a, b, (((1,), (1,)), ((), ())), precision=precision, preferred_element_type=F32
+    )
+
+
+def tn(a, b, precision=None):
+    return lax.dot_general(
+        a, b, (((0,), (0,)), ((), ())), precision=precision, preferred_element_type=F32
+    )
+
+
+def halves(values):
+    high = values.astype(BF16)
+    return high, (values - high.astype(F32)).astype(BF16)
+
+
+def pack_rows(single, frames, packed_ref):
+    width = single.shape[1]
+    high = frames.astype(BF16).astype(F32)
+    rest = frames - high
+    middle = rest.astype(BF16).astype(F32)
+    low = rest - middle
+    packed_ref[:, :width] = single.astype(BF16)
+    packed_ref[:, width:] = (
+        high + pltpu.roll(middle, 12, 1) + pltpu.roll(low, 24, 1)
+    ).astype(BF16)
+
+
+def unpack_frames(parts):
+    return parts + pltpu.roll(parts, 128 - 12, 1) + pltpu.roll(parts, 128 - 24, 1)
+
+
+def lane_eye(rows):
+    return (
+        lax.broadcasted_iota(jnp.int32, (rows, 128), 0)
+        == lax.broadcasted_iota(jnp.int32, (rows, 128), 1)
+    ).astype(F32)
+
+
+def start_kernel(single_ref, frames_ref, frames_out, packed_ref):
+    frames = tn(frames_ref[...], lane_eye(12), HIGHEST)
+    frames_out[...] = frames
+    pack_rows(single_ref[...], frames, packed_ref)
+
+
+def gather_kernel(n, packed_ref, all_ref, held, send_sems, recv_sems):
+    me = lax.axis_index("rows")
+    barrier = pltpu.get_barrier_semaphore()
+    for step in range(1, n):
+        pl.semaphore_signal(
+            barrier, inc=1, device_id={"rows": lax.rem(me + step, n)}, device_id_type=MESH_ID
+        )
+    pl.semaphore_wait(barrier, n - 1)
+    copies = []
+    for step in range(1, n):
+        copy = pltpu.make_async_remote_copy(
+            src_ref=packed_ref,
+            dst_ref=held.at[me],
+            send_sem=send_sems.at[step],
+            recv_sem=recv_sems.at[step],
+            device_id={"rows": lax.rem(me + step, n)},
+            device_id_type=MESH_ID,
+        )
+        copy.start()
+        copies.append(copy)
+    held[me] = packed_ref[...]
+    for copy in copies:
+        copy.wait()
+    all_ref[...] = held[...]
+
+
+def cycle_kernel(
+    cycle,
+    last,
+    sizes,
+    mask_smem,
+    chain_smem,
+    scale_smem,
+    all_ref,
+    single_ref,
+    frames_ref,
+    pair_ref,
+    bins_ref,
+    mask_ref,
+    chain_ref,
+    w_left,
+    w_right,
+    dist_embed,
+    chain_embed,
+    pair_gain,
+    mlp_in,
+    mlp_bias,
+    mlp_out,
+    w_qkv,
+    w_points,
+    bias_weight,
+    w_out,
+    single_gain,
+    w_frame,
+    head_mask,
+    key_mask,
+    shift_ref,
+    pick_ref,
+    pair_out,
+    single_out,
+    frames_out,
+    *rest,
+):
+    packed_ref = None if last else rest[0]
+    table_ref, sums_ref = rest[-2:]
+    head_count, head_dim, point_count = sizes
+    row_count, key_count, channels = pair_ref.shape
+    width = single_ref.shape[1]
+    bin_count = dist_embed.shape[0]
+    padded = head_mask.shape[0]
+    part = head_count * head_dim
+    block = head_count * point_count
+    me = lax.axis_index("rows")
+
+    table_ref[...] = jnp.zeros_like(table_ref)
+    table_ref[0:bin_count, :] = dist_embed[...].astype(F32)
+    table_ref[bin_count : bin_count + 2, :] = chain_embed[...].astype(F32)
+    table = table_ref[...].astype(BF16)
+
+    everyone = all_ref[...].astype(F32).reshape(key_count, all_ref.shape[2])
+    all_single = everyone[:, :width].astype(BF16)
+    key_frames = unpack_frames(everyone[:, width:])
+    single = single_ref[...]
+    own_single = single.astype(BF16)
+    frames = frames_ref[...]
+
+    left = nn(own_single, w_left[...])
+    right = nn(all_single, w_right[...]).astype(BF16).astype(F32)
+    key_live = mask_ref[...] > 0
+    live_rows = jnp.where(
+        (lax.broadcasted_iota(jnp.int32, (16, key_count), 0) == 0) & key_live, 1.0, 0.0
+    ).astype(BF16)
+    live_column = tn(live_rows, jnp.ones((16, channels), BF16))
+    gain = pair_gain[...]
+    bias_rows = nt(
+        (
+            lax.broadcasted_iota(jnp.int32, (padded, head_count), 0)
+            == lax.broadcasted_iota(jnp.int32, (padded, head_count), 1)
+        ).astype(BF16),
+        bias_weight[...],
+    ).astype(BF16)
+    levels = lax.broadcasted_iota(jnp.int32, (table_ref.shape[0], key_count), 0)
+    biases = []
+    for i in range(row_count):
+        live_i = mask_smem[me * row_count + i].astype(F32)
+        same = jnp.where(
+            chain_ref[...] == chain_smem[me * row_count + i], bin_count + 1, bin_count
+        )
+        onehot = jnp.where(
+            (levels == bins_ref[cycle, i : i + 1, :]) | (levels == same), 1.0, 0.0
+        ).astype(BF16)
+        mask_i = live_column * live_i
+        summed = (
+            pair_ref[i].astype(F32) + mask_i * (left[i : i + 1, :] + right) + tn(onehot, table)
+        )
+        normed = layer_norm(summed, gain).astype(BF16)
+        hidden = jnp.maximum(nn(normed, mlp_in[...]) + mlp_bias[...], 0.0).astype(BF16)
+        new_pair = (summed + mask_i * nn(hidden, mlp_out[...])).astype(BF16)
+        pair_out[i] = new_pair
+        biases.append(nt(bias_rows, new_pair))
+    biases = jnp.concatenate(biases, axis=0)
+
+    def spread_heads(values, mask):
+        return jnp.concatenate([values[i : i + 1, :] * mask for i in range(row_count)], axis=0)
+
+    def gather_heads(values, mask):
+        return jnp.sum(
+            values.reshape(row_count, padded, values.shape[1]) * mask[None, :, :], axis=1
+        )
+
+    heads = head_mask[...]
+    key_slots = key_mask[...]
+    queries = nn(own_single, w_qkv[:, 0:part]).astype(BF16)
+    keys = nn(all_single, w_qkv[:, part : 2 * part]).astype(BF16)
+    values = nn(all_single, w_qkv[:, 2 * part : 3 * part]).astype(BF16)
+    scores = nt(spread_heads(queries.astype(F32), heads[:, :part]).astype(BF16), keys)
+
+    own_local = []
+    key_local = []
+    for axis in range(3):
+        weight = w_points[:, axis * block : (axis + 1) * block]
+        own_local.append(nn(own_single, weight))
+        key_local.append(nn(all_single, weight))
+
+    def globals_of(points, turns):
+        return [
+            turns[:, 3 * a : 3 * a + 1] * points[0]
+            + turns[:, 3 * a + 1 : 3 * a + 2] * points[1]
+            + turns[:, 3 * a + 2 : 3 * a + 3] * points[2]
+            + turns[:, 9 + a : 10 + a]
+            for a in range(3)
+        ]
+
+    own_global = globals_of(own_local, frames)
+    key_global = globals_of(key_local, key_frames)
+    shift = shift_ref[...]
+    cross = jnp.zeros((row_count * padded, key_count), F32)
+    query_sq = jnp.zeros((row_count * padded, 1), F32)
+    square = jnp.zeros((key_count, block), F32)
+    key_halves = []
+    for a in range(3):
+        query = spread_heads(nn(own_global[a], shift, HIGHEST), key_slots)
+        query_sq = query_sq + jnp.sum(query * query, axis=1, keepdims=True)
+        square = square + key_global[a] * key_global[a]
+        query_high, query_low = halves(query)
+        key_high, key_low = halves(key_global[a])
+        key_halves.append((key_high, key_low))
+        cross = cross + nt(query_high, key_high) + nt(query_low, key_high) + nt(query_high, key_low)
+    square_high, square_low = halves(square)
+    slots_bf = key_slots.astype(BF16)
+    key_sq = nt(slots_bf, square_high) + nt(slots_bf, square_low)
+    distance = query_sq + jnp.concatenate([key_sq] * row_count, axis=0) - 2.0 * cross
+    point_weight = math.sqrt(2.0 / (9.0 * NQP)) / 2.0
+    head_rows = lax.broadcasted_iota(jnp.int32, (padded, key_count), 0)
+    scale = jnp.zeros((padded, key_count), F32)
+    for h in range(head_count):
+        scale = jnp.where(head_rows == h, scale_smem[h] * point_weight, scale)
+    scale = jnp.concatenate([scale] * row_count, axis=0)
+    logits = math.sqrt(1.0 / 3.0) * (scores * head_dim ** (-0.5) + biases - scale * distance)
+    logits = jnp.where(key_live, logits, -1e30)
+    top = jnp.max(logits, axis=1, keepdims=True)
+    weights = jnp.where(key_live, jnp.exp(logits - top), 0.0).astype(BF16)
+    inverse = 1.0 / jnp.sum(weights.astype(F32), axis=1, keepdims=True)
+
+    attended = gather_heads(nn(weights, values) * inverse, heads[:, :part])
+    centred = [
+        gather_heads((nn(weights, key_halves[a][0]) + nn(weights, key_halves[a][1])) * inverse, heads)
+        - frames[:, 9 + a : 10 + a]
+        for a in range(3)
+    ]
+    local = [
+        frames[:, b : b + 1] * centred[0]
+        + frames[:, 3 + b : 4 + b] * centred[1]
+        + frames[:, 6 + b : 7 + b] * centred[2]
+        for b in range(3)
+    ]
+    lengths = jnp.sqrt(local[0] * local[0] + local[1] * local[1] + local[2] * local[2] + 1.0)
+    update = nn(attended.astype(BF16), w_out[0:part, :])
+    count = pick_ref.shape[1]
+    for a, item in enumerate(local + [lengths]):
+        picked = nn(item.astype(BF16), pick_ref[...]).astype(BF16)
+        update = update + nn(picked, w_out[part + a * count : part + (a + 1) * count, :])
+    for i in range(row_count):
+        rows = slice(i * padded, (i + 1) * padded)
+        sums_ref[i] = nn(weights[rows, :], pair_out[i]) * inverse[rows, :]
+    pair_sums = jnp.concatenate(
+        [sums_ref[:, h, :].astype(BF16) for h in range(head_count)], axis=1
+    )
+    update = update + nn(pair_sums, w_out[part + 4 * count :, :])
+    single = layer_norm(single + update, single_gain[...])
+    single_out[...] = single
+    step = nn(single.astype(BF16), w_frame[...])
+    quat = [step[:, k : k + 1] for k in range(3)]
+    quat_a = lax.rsqrt(1.0 + (quat[0] * quat[0] + quat[1] * quat[1] + quat[2] * quat[2]))
+    quat_b, quat_c, quat_d = (q * quat_a for q in quat)
+    turn = [
+        quat_a * quat_a + quat_b * quat_b - quat_c * quat_c - quat_d * quat_d,
+        2.0 * (quat_b * quat_c - quat_a * quat_d),
+        2.0 * (quat_b * quat_d + quat_a * quat_c),
+        2.0 * (quat_b * quat_c + quat_a * quat_d),
+        quat_a * quat_a - quat_b * quat_b + quat_c * quat_c - quat_d * quat_d,
+        2.0 * (quat_c * quat_d - quat_a * quat_b),
+        2.0 * (quat_b * quat_d - quat_a * quat_c),
+        2.0 * (quat_c * quat_d + quat_a * quat_b),
+        quat_a * quat_a - quat_b * quat_b - quat_c * quat_c + quat_d * quat_d,
+    ]
+    column = [frames[:, k : k + 1] for k in range(12)]
+    lanes = lax.broadcasted_iota(jnp.int32, (row_count, 128), 1)
+    new_frames = jnp.zeros((row_count, 128), F32)
+    for a in range(3):
+        for c in range(3):
+            entry = (
+                column[3 * a] * turn[c]
+                + column[3 * a + 1] * turn[3 + c]
+                + column[3 * a + 2] * turn[6 + c]
+            )
+            new_frames = jnp.where(lanes == 3 * a + c, entry, new_frames)
+        entry = (
+            column[3 * a] * step[:, 3:4]
+            + column[3 * a + 1] * step[:, 4:5]
+            + column[3 * a + 2] * step[:, 5:6]
+            + column[9 + a]
+        )
+        new_frames = jnp.where(lanes == 9 + a, entry, new_frames)
+    if last:
+        frames_out[...] = nt(lane_eye(12), new_frames, HIGHEST)
+    else:
+        frames_out[...] = new_frames
+        pack_rows(single, new_frames, packed_ref)
+
+
+def tables(head_count, head_dim, point_count):
+    padded = -(-head_count // 16) * 16
+    value_count = point_count - 2 * NQP
+    row = np.arange(padded)[:, None]
+    lane = np.arange(head_count * point_count)[None, :]
+    heads = (row == lane // point_count).astype(np.float32)
+    slot = lane % point_count
+    key_slots = heads * ((slot >= NQP) & (slot < 2 * NQP))
+    lanes = np.arange(head_count * point_count)
+    shift = (lanes[:, None] + NQP == lanes[None, :]).astype(np.float32)
+    picked = np.arange(head_count * value_count)
+    source = picked // value_count * point_count + 2 * NQP + picked % value_count
+    pick = (lanes[:, None] == source[None, :]).astype(np.float32)
+    return heads, key_slots.astype(np.float32), shift, jnp.asarray(pick, BF16)
+
+
+def dense_shards(
+    ring,
+    pair_in,
+    single_in,
+    frames_in,
+    dist_bins,
+    res_mask,
+    chain_ids,
+    w_left,
+    w_right,
+    dist_embed,
+    chain_embed,
+    pair_gain,
+    mlp_in,
+    mlp_bias,
+    mlp_out,
+    w_qkv,
+    w_points,
+    bias_weight,
+    point_scale,
+    w_out,
+    single_gain,
+    w_frame,
+):
+    row_count, key_count, channels = pair_in.shape
+    width = single_in.shape[1]
+    head_count = bias_weight.shape[1]
+    head_dim = w_qkv.shape[1] // (3 * head_count)
+    point_count = w_points.shape[1] // (3 * head_count)
+    heads, key_slots, shift, pick = tables(head_count, head_dim, point_count)
+    padded = heads.shape[0]
+    vmem = pl.BlockSpec(memory_space=pltpu.VMEM)
+    smem = pl.BlockSpec(memory_space=pltpu.SMEM)
+    packed_shape = jax.ShapeDtypeStruct((row_count, width + 128), BF16)
+    row_frames = jax.ShapeDtypeStruct((row_count, 128), F32)
+    frames, packed = pl.pallas_call(
+        start_kernel,
+        out_shape=(row_frames, packed_shape),
+        in_specs=[vmem] * 2,
+        out_specs=(vmem, vmem),
+        name="start",
+    )(single_in, frames_in)
+    pair, single = pair_in, single_in
+    for cycle in range(CYCLES):
+        last = cycle == CYCLES - 1
+        everyone = pl.pallas_call(
+            functools.partial(gather_kernel, ring),
+            out_shape=jax.ShapeDtypeStruct((ring, row_count, width + 128), BF16),
+            in_specs=[vmem],
+            out_specs=vmem,
+            scratch_shapes=[
+                pltpu.VMEM((ring, row_count, width + 128), BF16),
+                pltpu.SemaphoreType.DMA((ring,)),
+                pltpu.SemaphoreType.DMA((ring,)),
+            ],
+            compiler_params=pltpu.CompilerParams(collective_id=cycle, has_side_effects=True),
+            name=f"gather_{cycle}",
+        )(packed)
+        out_shape = [
+            jax.ShapeDtypeStruct(pair.shape, BF16),
+            jax.ShapeDtypeStruct(single.shape, F32),
+            jax.ShapeDtypeStruct(frames_in.shape, F32) if last else row_frames,
+        ]
+        if not last:
+            out_shape.append(packed_shape)
+        outs = pl.pallas_call(
+            functools.partial(cycle_kernel, cycle, last, (head_count, head_dim, point_count)),
+            out_shape=tuple(out_shape),
+            in_specs=[smem] * 3 + [vmem] * 25,
+            out_specs=(vmem,) * len(out_shape),
+            scratch_shapes=[
+                pltpu.VMEM((-(-(dist_embed.shape[0] + 2) // 16) * 16, channels), F32),
+                pltpu.VMEM((row_count, padded, channels), F32),
+            ],
+            name=f"cycle_{cycle}",
+        )(
+            res_mask,
+            chain_ids,
+            point_scale,
+            everyone,
+            single,
+            frames,
+            pair,
+            dist_bins,
+            res_mask.reshape(1, -1),
+            chain_ids.reshape(1, -1),
+            w_left,
+            w_right,
+            dist_embed,
+            chain_embed,
+            pair_gain.reshape(1, -1),
+            mlp_in,
+            mlp_bias.reshape(1, -1),
+            mlp_out,
+            w_qkv,
+            w_points,
+            bias_weight,
+            w_out,
+            single_gain.reshape(1, -1),
+            w_frame,
+            heads,
+            key_slots,
+            shift,
+            pick,
+        )
+        pair, single, frames = outs[:3]
+        packed = None if last else outs[3]
+    return pair, single, frames
+
+
 def solution(mesh):
     in_specs = (
         P(("groups", "rows"), "cols", None),
@@ -337,4 +775,7 @@
         P(("groups", "rows"), None),
         P(None, ("groups", "rows")),
     )
-    return jax.shard_map(shards, mesh=mesh, in_specs=in_specs, out_specs=out_specs, check_vma=False)
+    body = shards
+    if mesh.shape["cols"] == 1 and mesh.shape["rows"] > 1:
+        body = functools.partial(dense_shards, mesh.shape["rows"])
+    return jax.shard_map(body, mesh=mesh, in_specs=in_specs, out_specs=out_specs, check_vma=False)

time: 197 us -> 54.7 us (0.28)
  blocking collectives: 115 us -> 0 us
  Pallas kernels: 0 us -> 42.6 us
  matrix products: 35.8 us -> 0 us
  local copies, waits for them, and re-layouts: 30 us -> 10.9 us
  other arithmetic: 11.5 us -> 0 us
    all_gather x6 -> x0, blocking collectives: 115 us -> none  [the longest x2 40.7 us: shards(): lax.all_gather(own_right, 'rows', axis=0, tiled=True)]
    pallas_call x0 -> x5, Pallas kernels: none -> 42.6 us  [the longest x2 21.1 us: dense_shards(): pl.pallas_call(functools.partial(cycle_kernel, cycle, last, (head_count,...]
    dot_general x60 -> x0, matrix products: 35.2 us -> none  [the longest x16 15.4 us: update_row(): mixed_out = jnp.dot(hidden, mlp_out, preferred_element_type=jnp.float32)]
    convert_element_type x22 -> x0, other arithmetic: 8.24 us -> none  [the longest x16 5.94 us: update_row(): chain_embed[1].astype(jnp.float32)]
    dynamic_slice x17 -> x0, local copies, waits for them, and re-layouts: 7.75 us -> none  [the longest x16 7.02 us: shards(): lax.map(row_step, (pair_tile, dist_bins[cycle_index], left_proj, pair_mas...]
    unnamed x68 -> x5, local copies, waits for them, and re-layouts: 2.5 us -> 8.27 us
    eq x16 -> x0, local copies, waits for them, and re-layouts: 5.66 us -> none  [update_row(): bins_row[:, None]]
    mul x16 -> x0, local copies, waits for them, and re-layouts: 5.61 us -> none  [update_row(): mask_row[:, None] * (left_row[None, :] + right_keys.astype(jnp.float32))]
where the time goes in v1:
time: 54.7 us; the launch traced here: 54.1 us
  Pallas kernels  42.6 us (78%)
  local copies, waits for them, and re-layouts  10.9 us (20%)
  between operations  0.66 us (1%)
    pallas_call x2, Pallas kernels, dense_shards(): pl.pallas_call(functools.partial(cycle_kernel, cycle, last, (head_count,...  21.1 us
    pallas_call x2, Pallas kernels, dense_shards(): pl.pallas_call(functools.partial(gather_kernel, ring), out_shape=jax.Shap...  19.8 us
    unnamed x5, local copies, waits for them, and re-layouts  8.27 us
    pallas_call x1, Pallas kernels, dense_shards(): pl.pallas_call(start_kernel, out_shape=(row_frames, packed_shape), in_spe...  1.59 us
    pallas_call x1, local copies, waits for them, and re-layouts, dense_shards(): pl.pallas_call(functools.partial(cycle_kernel, cycle, last, (head_count,...  1.36 us
    reshape x1, local copies, waits for them, and re-layouts, dense_shards(): single_gain.reshape(1, -1)  1.25 us

profile of v1, /device:TPU:0, one launch (start us, length us, event | category | flops | bytes accessed | tf_op | source)
XLA Modules:
  0.0 54.1 jit_solution(7174583373373669536)
XLA Ops:
  0.6 1.2 %reshape.30.single_gain = f32[1,384]{1,0:T(1,128)} reshape(f32[384]{0:T(512)} %param.44) | data formatting | bytes 3072 | tf_op jit(solution)/shard_map/reshape | solution.py:737
  1.9 1.4 %copy.28.frames_ref = f32[12,8]{1,0:T(8,128)} copy(f32[12,8]{0,1:T(8,128)} %param.27) | data formatting | bytes 768 | tf_op args[2]
  3.2 1.6 %start.1 = (f32[8,128]{1,0:T(8,128)}, bf16[8,512]{1,0:T(8,128)(2,1)}) custom-call(f32[8,384]{1,0:T(8,128)} %single_ref.3, f32[12,8]{1,0:T(8,128)} %copy.28.frames_ref), custom_call_target="tpu_custom_call" | custom-call | tf_op jit(solution)/shard_map/start/pallas_call | solution.py:674
  4.8 1.4 %copy.31.bias_weight = bf16[128,12]{1,0:T(8,128)(2,1)} copy(bf16[128,12]{0,1:T(8,128)(2,1)} %param.41) | data formatting | bytes 6144 | tf_op args[16]
  6.2 1.5 %copy.32.w_frame = bf16[384,6]{1,0:T(8,128)(2,1)} copy(bf16[384,6]{0,1:T(8,128)(2,1)} %param.45) | data formatting | bytes 9216 | tf_op args[20]
  7.7 10.5 %gather_0.1.all_ref = bf16[16,8,512]{2,1,0:T(8,128)(2,1)} custom-call(bf16[8,512]{1,0:T(8,128)(2,1)} %get-tuple-element.9.packed_ref), custom_call_target="tpu_custom_call" | custom-call | tf_op jit(solution)/shard_map/gather_0/pallas_call | solution.py:684
  18.2 2.0 %copy.29.w_qkv = bf16[384,576]{1,0:T(8,128)(2,1)} copy(bf16[384,576]{0,1:T(8,128)(2,1)} %param.39) | data formatting | bytes 884736 | tf_op args[14]
  20.2 2.0 %copy.30.w_points = bf16[384,576]{1,0:T(8,128)(2,1)} copy(bf16[384,576]{0,1:T(8,128)(2,1)} %param.40) | data formatting | bytes 884736 | tf_op args[15]
  22.2 10.9 %cycle_0.1 = (bf16[8,128,128]{2,1,0:T(8,128)(2,1)}, f32[8,384]{1,0:T(8,128)}, f32[8,128]{1,0:T(8,128)}, bf16[8,512]{1,0:T(8,128)(2,1)}) custom-call(s32[128]{0:T(128)} %mask_smem.3, s32[128]{0:T(128)} %chain_smem.3, f32[12]{0:T(128)} %scale_smem.3, bf16[16,8,512]{2,1,0:T(8,128)(2,1)} %gather_0.1.all_ref, f32[8,384]{1,0:T(8,128)} %single_ref.3, ...), custom_call_target="tpu_custom_call" | custom-call | tf_op jit(solution)/shard_map/cycle_0/pallas_call | solution.py:704
  33.2 9.4 %gather_1.1.all_ref = bf16[16,8,512]{2,1,0:T(8,128)(2,1)} custom-call(bf16[8,512]{1,0:T(8,128)(2,1)} %get-tuple-element.11.packed_ref), custom_call_target="tpu_custom_call" | custom-call | tf_op jit(solution)/shard_map/gather_1/pallas_call | solution.py:684
  42.5 10.2 %cycle_1.1 = (bf16[8,128,128]{2,1,0:T(8,128)(2,1)}, f32[8,384]{1,0:T(8,128)}, f32[12,8]{1,0:T(8,128)}) custom-call(s32[128]{0:T(128)} %mask_smem.3, s32[128]{0:T(128)} %chain_smem.3, f32[12]{0:T(128)} %scale_smem.3, bf16[16,8,512]{2,1,0:T(8,128)(2,1)} %gather_1.1.all_ref, f32[8,384]{1,0:T(8,128)} %get-tuple-element.12.single_ref, ...), custom_call_target="tpu_custom_call" | custom-call | tf_op jit(solution)/shard_map/cycle_1/pallas_call | solution.py:704
  52.7 1.4 %copy.37 = f32[12,8]{0,1:T(8,128)} copy(f32[12,8]{1,0:T(8,128)} %get-tuple-element.17) | data formatting | bytes 768 | tf_op jit(solution)/shard_map/cycle_1/pallas_call | solution.py:704

commit v2 on v0

--- a/solution.py
+++ b/solution.py
@@ -1,8 +1,12 @@
+import functools
 import math
 
 import jax
 import jax.numpy as jnp
+import numpy as np
 from jax import lax
+from jax.experimental import pallas as pl
+from jax.experimental.pallas import tpu as pltpu
 from jax.sharding import PartitionSpec as P
 
 NQP = 4
@@ -308,6 +312,457 @@
     return (pair_tile, single, frames.T)
 
 
+BF16 = jnp.bfloat16
+F32 = jnp.float32
+MESH_ID = pl.DeviceIdType.MESH
+
+
+def nn(a, b, precision=None):
+    return lax.dot_general(
+        a, b, (((1,), (0,)), ((), ())), precision=precision, preferred_element_type=F32
+    )
+
+
+def nt(a, b, precision=None):
+    return lax.dot_general(
+        a, b, (((1,), (1,)), ((), ())), precision=precision, preferred_element_type=F32
+    )
+
+
+def tn(a, b, precision=None):
+    return lax.dot_general(
+        a, b, (((0,), (0,)), ((), ())), precision=precision, preferred_element_type=F32
+    )
+
+
+def halves(values):
+    high = values.astype(BF16)
+    return high, (values - high.astype(F32)).astype(BF16)
+
+
+def pack_rows(single, frames, packed_ref):
+    width = single.shape[1]
+    high = frames.astype(BF16).astype(F32)
+    rest = frames - high
+    middle = rest.astype(BF16).astype(F32)
+    low = rest - middle
+    packed_ref[:, :width] = single.astype(BF16)
+    packed_ref[:, width:] = (
+        high + pltpu.roll(middle, 12, 1) + pltpu.roll(low, 24, 1)
+    ).astype(BF16)
+
+
+def unpack_frames(parts):
+    return parts + pltpu.roll(parts, 128 - 12, 1) + pltpu.roll(parts, 128 - 24, 1)
+
+
+def lane_eye(rows):
+    return (
+        lax.broadcasted_iota(jnp.int32, (rows, 128), 0)
+        == lax.broadcasted_iota(jnp.int32, (rows, 128), 1)
+    ).astype(F32)
+
+
+IN_PLACE = (
+    "mask_smem",
+    "chain_smem",
+    "scale_smem",
+    "single_in",
+    "frames_in",
+    "bins",
+    "mask",
+    "chain",
+    "w_left",
+    "w_right",
+    "dist_embed",
+    "chain_embed",
+    "pair_gain",
+    "mlp_bias",
+    "bias_weight",
+    "single_gain",
+    "w_frame",
+    "head_mask",
+    "key_mask",
+    "shift",
+    "pick",
+)
+FETCHED = ("pair_in", "w_qkv", "w_points", "mlp_in", "mlp_out", "w_out")
+SCRATCH = (
+    "send",
+    "held",
+    "table",
+    "sums",
+    "base",
+    "send_sems",
+    "recv_sems",
+    "fetch_sems",
+)
+
+
+def cycles_kernel(ring, sizes, *refs):
+    names = IN_PLACE + FETCHED
+    r = dict(zip(names, refs))
+    refs = refs[len(names) :]
+    pair_out, single_out, frames_out = refs[:3]
+    s = dict(zip(FETCHED + SCRATCH, refs[3:]))
+    head_count, head_dim, point_count = sizes
+    row_count, key_count, channels = pair_out.shape
+    width = single_out.shape[1]
+    bin_count = r["dist_embed"].shape[0]
+    padded = r["head_mask"].shape[0]
+    part = head_count * head_dim
+    block = head_count * point_count
+    me = lax.axis_index("rows")
+
+    barrier = pltpu.get_barrier_semaphore()
+    for step in range(1, ring):
+        pl.semaphore_signal(
+            barrier, inc=1, device_id={"rows": lax.rem(me + step, ring)}, device_id_type=MESH_ID
+        )
+    fetches = {}
+    for k, name in enumerate(FETCHED):
+        fetches[name] = pltpu.make_async_copy(r[name], s[name], s["fetch_sems"].at[k])
+        fetches[name].start()
+
+    def send(cycle):
+        copies = []
+        for step in range(1, ring):
+            copy = pltpu.make_async_remote_copy(
+                src_ref=s["send"].at[cycle],
+                dst_ref=s["held"].at[cycle, me],
+                send_sem=s["send_sems"].at[cycle, step],
+                recv_sem=s["recv_sems"].at[cycle, step],
+                device_id={"rows": lax.rem(me + step, ring)},
+                device_id_type=MESH_ID,
+            )
+            copy.start()
+            copies.append(copy)
+        s["held"][cycle, me] = s["send"][cycle]
+        return copies
+
+    single = r["single_in"][...]
+    frames = nn(r["frames_in"][...], lane_eye(r["frames_in"].shape[1]), HIGHEST)
+    pack_rows(single, frames, s["send"].at[0])
+    pl.semaphore_wait(barrier, ring - 1)
+    copies = send(0)
+
+    s["table"][...] = jnp.zeros_like(s["table"])
+    s["table"][0:bin_count, :] = r["dist_embed"][...].astype(F32)
+    s["table"][bin_count : bin_count + 2, :] = r["chain_embed"][...].astype(F32)
+    table = s["table"][...].astype(BF16)
+    key_live = r["mask"][...].reshape(1, key_count) > 0
+    chain = r["chain"][...].reshape(1, key_count)
+    live_rows = jnp.where(
+        (lax.broadcasted_iota(jnp.int32, (16, key_count), 0) == 0) & key_live, 1.0, 0.0
+    ).astype(BF16)
+    live_column = tn(live_rows, jnp.ones((16, channels), BF16))
+    gain = r["pair_gain"][...].reshape(1, channels)
+    mlp_bias = r["mlp_bias"][...].reshape(1, -1)
+    single_gain = r["single_gain"][...].reshape(1, width)
+    bias_rows = nn(
+        (
+            lax.broadcasted_iota(jnp.int32, (padded, head_count), 0)
+            == lax.broadcasted_iota(jnp.int32, (padded, head_count), 1)
+        ).astype(BF16),
+        r["bias_weight"][...],
+    ).astype(BF16)
+    levels = lax.broadcasted_iota(jnp.int32, (s["table"].shape[0], key_count), 0)
+    heads = r["head_mask"][...]
+    key_slots = r["key_mask"][...]
+    slots_bf = key_slots.astype(BF16)
+    shift = r["shift"][...]
+    head_rows = lax.broadcasted_iota(jnp.int32, (padded, key_count), 0)
+    point_weight = math.sqrt(2.0 / (9.0 * NQP)) / 2.0
+    scale = jnp.zeros((padded, key_count), F32)
+    for h in range(head_count):
+        scale = jnp.where(head_rows == h, r["scale_smem"][h] * point_weight, scale)
+    scale = jnp.concatenate([scale] * row_count, axis=0)
+
+    def mask_of(i):
+        return live_column * r["mask_smem"][me * row_count + i].astype(F32)
+
+    def spread_heads(values, mask):
+        return jnp.concatenate([values[i : i + 1, :] * mask for i in range(row_count)], axis=0)
+
+    def gather_heads(values, mask):
+        return jnp.sum(
+            values.reshape(row_count, padded, values.shape[1]) * mask[None, :, :], axis=1
+        )
+
+    def globals_of(points, turns):
+        return [
+            turns[:, 3 * a : 3 * a + 1] * points[0]
+            + turns[:, 3 * a + 1 : 3 * a + 2] * points[1]
+            + turns[:, 3 * a + 2 : 3 * a + 3] * points[2]
+            + turns[:, 9 + a : 10 + a]
+            for a in range(3)
+        ]
+
+    for cycle in range(CYCLES):
+        last = cycle == CYCLES - 1
+        own_single = single.astype(BF16)
+        left = nn(own_single, r["w_left"][...])
+        if cycle == 0:
+            fetches["pair_in"].wait()
+        old_pair = s["pair_in"] if cycle == 0 else pair_out
+        for i in range(row_count):
+            same = jnp.where(
+                chain == r["chain_smem"][me * row_count + i], bin_count + 1, bin_count
+            )
+            onehot = jnp.where(
+                (levels == r["bins"][cycle, i : i + 1, :]) | (levels == same), 1.0, 0.0
+            ).astype(BF16)
+            s["base"][i] = (
+                old_pair[i].astype(F32) + mask_of(i) * left[i : i + 1, :] + tn(onehot, table)
+            )
+        if cycle == 0:
+            fetches["w_qkv"].wait()
+            fetches["w_points"].wait()
+        queries = nt(own_single, s["w_qkv"][0:part, :]).astype(BF16)
+        spread_queries = spread_heads(queries.astype(F32), heads[:, :part]).astype(BF16)
+        own_global = globals_of(
+            [
+                nt(own_single, s["w_points"][axis * block : (axis + 1) * block, :])
+                for axis in range(3)
+            ],
+            frames,
+        )
+        query_sq = jnp.zeros((row_count * padded, 1), F32)
+        query_halves = []
+        for a in range(3):
+            query = spread_heads(nn(own_global[a], shift, HIGHEST), key_slots)
+            query_sq = query_sq + jnp.sum(query * query, axis=1, keepdims=True)
+            query_halves.append(halves(query))
+        if cycle == 0:
+            fetches["mlp_in"].wait()
+            fetches["mlp_out"].wait()
+            fetches["w_out"].wait()
+        for copy in copies:
+            copy.wait()
+
+        everyone = s["held"][cycle].astype(F32).reshape(key_count, width + 128)
+        all_single = everyone[:, :width].astype(BF16)
+        key_frames = unpack_frames(everyone[:, width:])
+        right = nn(all_single, r["w_right"][...]).astype(BF16).astype(F32)
+        biases = []
+        for i in range(row_count):
+            mask_i = mask_of(i)
+            summed = s["base"][i] + mask_i * right
+            normed = layer_norm(summed, gain).astype(BF16)
+            hidden = jnp.maximum(nn(normed, s["mlp_in"][...]) + mlp_bias, 0.0).astype(BF16)
+            new_pair = (summed + mask_i * nn(hidden, s["mlp_out"][...])).astype(BF16)
+            pair_out[i] = new_pair
+            biases.append(nt(bias_rows, new_pair))
+        biases = jnp.concatenate(biases, axis=0)
+
+        keys = nt(all_single, s["w_qkv"][part : 2 * part, :]).astype(BF16)
+        values = nt(all_single, s["w_qkv"][2 * part : 3 * part, :]).astype(BF16)
+        scores = nt(spread_queries, keys)
+        key_global = globals_of(
+            [
+                nt(all_single, s["w_points"][axis * block : (axis + 1) * block, :])
+                for axis in range(3)
+            ],
+            key_frames,
+        )
+        cross = jnp.zeros((row_count * padded, key_count), F32)
+        square = jnp.zeros((key_count, block), F32)
+        key_halves = []
+        for a in range(3):
+            square = square + key_global[a] * key_global[a]
+            query_high, query_low = query_halves[a]
+            key_high, key_low = halves(key_global[a])
+            key_halves.append((key_high, key_low))
+            cross = (
+                cross
+                + nt(query_high, key_high)
+                + nt(query_low, key_high)
+                + nt(query_high, key_low)
+            )
+        square_high, square_low = halves(square)
+        key_sq = nt(slots_bf, square_high) + nt(slots_bf, square_low)
+        distance = query_sq + jnp.concatenate([key_sq] * row_count, axis=0) - 2.0 * cross
+        logits = math.sqrt(1.0 / 3.0) * (scores * head_dim ** (-0.5) + biases - scale * distance)
+        logits = jnp.where(key_live, logits, -1e30)
+        top = jnp.max(logits, axis=1, keepdims=True)
+        weights = jnp.where(key_live, jnp.exp(logits - top), 0.0).astype(BF16)
+        inverse = 1.0 / jnp.sum(weights.astype(F32), axis=1, keepdims=True)
+
+        attended = gather_heads(nn(weights, values) * inverse, heads[:, :part])
+        centred = [
+            gather_heads(
+                (nn(weights, key_halves[a][0]) + nn(weights, key_halves[a][1])) * inverse, heads
+            )
+            - frames[:, 9 + a : 10 + a]
+            for a in range(3)
+        ]
+        local = [
+            frames[:, b : b + 1] * centred[0]
+            + frames[:, 3 + b : 4 + b] * centred[1]
+            + frames[:, 6 + b : 7 + b] * centred[2]
+            for b in range(3)
+        ]
+        lengths = jnp.sqrt(
+            local[0] * local[0] + local[1] * local[1] + local[2] * local[2] + 1.0
+        )
+        w_out = s["w_out"]
+        update = nn(attended.astype(BF16), w_out[0:part, :])
+        count = r["pick"].shape[1]
+        for a, item in enumerate(local + [lengths]):
+            picked = nn(item.astype(BF16), r["pick"][...]).astype(BF16)
+            update = update + nn(picked, w_out[part + a * count : part + (a + 1) * count, :])
+        for i in range(row_count):
+            rows = slice(i * padded, (i + 1) * padded)
+            s["sums"][i] = nn(weights[rows, :], pair_out[i]) * inverse[rows, :]
+        pair_sums = jnp.concatenate(
+            [s["sums"][:, h, :].astype(BF16) for h in range(head_count)], axis=1
+        )
+        update = update + nn(pair_sums, w_out[part + 4 * count :, :])
+        single = layer_norm(single + update, single_gain)
+        frames = next_frames(frames, nt(single.astype(BF16), r["w_frame"][...]))
+        if not last:
+            pack_rows(single, frames, s["send"].at[cycle + 1])
+            copies = send(cycle + 1)
+    single_out[...] = single
+    frames_out[...] = frames[:, : frames_out.shape[1]]
+
+
+def next_frames(frames, step):
+    quat = [step[:, k : k + 1] for k in range(3)]
+    quat_a = lax.rsqrt(1.0 + (quat[0] * quat[0] + quat[1] * quat[1] + quat[2] * quat[2]))
+    quat_b, quat_c, quat_d = (q * quat_a for q in quat)
+    turn = [
+        quat_a * quat_a + quat_b * quat_b - quat_c * quat_c - quat_d * quat_d,
+        2.0 * (quat_b * quat_c - quat_a * quat_d),
+        2.0 * (quat_b * quat_d + quat_a * quat_c),
+        2.0 * (quat_b * quat_c + quat_a * quat_d),
+        quat_a * quat_a - quat_b * quat_b + quat_c * quat_c - quat_d * quat_d,
+        2.0 * (quat_c * quat_d - quat_a * quat_b),
+        2.0 * (quat_b * quat_d - quat_a * quat_c),
+        2.0 * (quat_c * quat_d + quat_a * quat_b),
+        quat_a * quat_a - quat_b * quat_b - quat_c * quat_c + quat_d * quat_d,
+    ]
+    column = [frames[:, k : k + 1] for k in range(12)]
+    lanes = lax.broadcasted_iota(jnp.int32, frames.shape, 1)
+    new_frames = jnp.zeros(frames.shape, F32)
+    for a in range(3):
+        for c in range(3):
+            entry = (
+                column[3 * a] * turn[c]
+                + column[3 * a + 1] * turn[3 + c]
+                + column[3 * a + 2] * turn[6 + c]
+            )
+            new_frames = jnp.where(lanes == 3 * a + c, entry, new_frames)
+        entry = (
+            column[3 * a] * step[:, 3:4]
+            + column[3 * a + 1] * step[:, 4:5]
+            + column[3 * a + 2] * step[:, 5:6]
+            + column[9 + a]
+        )
+        new_frames = jnp.where(lanes == 9 + a, entry, new_frames)
+    return new_frames
+
+
+def tables(head_count, head_dim, point_count):
+    padded = -(-head_count // 16) * 16
+    value_count = point_count - 2 * NQP
+    row = np.arange(padded)[:, None]
+    lane = np.arange(head_count * point_count)[None, :]
+    heads = (row == lane // point_count).astype(np.float32)
+    slot = lane % point_count
+    key_slots = heads * ((slot >= NQP) & (slot < 2 * NQP))
+    lanes = np.arange(head_count * point_count)
+    shift = (lanes[:, None] + NQP == lanes[None, :]).astype(np.float32)
+    picked = np.arange(head_count * value_count)
+    source = picked // value_count * point_count + 2 * NQP + picked % value_count
+    pick = (lanes[:, None] == source[None, :]).astype(np.float32)
+    return heads, key_slots.astype(np.float32), shift, jnp.asarray(pick, BF16)
+
+
+def dense_shards(
+    ring,
+    pair_in,
+    single_in,
+    frames_in,
+    dist_bins,
+    res_mask,
+    chain_ids,
+    w_left,
+    w_right,
+    dist_embed,
+    chain_embed,
+    pair_gain,
+    mlp_in,
+    mlp_bias,
+    mlp_out,
+    w_qkv,
+    w_points,
+    bias_weight,
+    point_scale,
+    w_out,
+    single_gain,
+    w_frame,
+):
+    row_count, key_count, channels = pair_in.shape
+    width = single_in.shape[1]
+    head_count = bias_weight.shape[1]
+    head_dim = w_qkv.shape[1] // (3 * head_count)
+    point_count = w_points.shape[1] // (3 * head_count)
+    heads, key_slots, shift, pick = tables(head_count, head_dim, point_count)
+    padded = heads.shape[0]
+    vmem = pl.BlockSpec(memory_space=pltpu.VMEM)
+    smem = pl.BlockSpec(memory_space=pltpu.SMEM)
+    anywhere = pl.BlockSpec(memory_space=pl.ANY)
+    fetched = (pair_in, w_qkv.T, w_points.T, mlp_in, mlp_out, w_out)
+    pair, single, frames = pl.pallas_call(
+        functools.partial(cycles_kernel, ring, (head_count, head_dim, point_count)),
+        out_shape=(
+            jax.ShapeDtypeStruct(pair_in.shape, BF16),
+            jax.ShapeDtypeStruct(single_in.shape, F32),
+            jax.ShapeDtypeStruct(frames_in.shape[::-1], F32),
+        ),
+        in_specs=[smem] * 3 + [vmem] * (len(IN_PLACE) - 3) + [anywhere] * len(FETCHED),
+        out_specs=(vmem,) * 3,
+        scratch_shapes=[pltpu.VMEM(item.shape, item.dtype) for item in fetched]
+        + [
+            pltpu.VMEM((CYCLES, row_count, width + 128), BF16),
+            pltpu.VMEM((CYCLES, ring, row_count, width + 128), BF16),
+            pltpu.VMEM((-(-(dist_embed.shape[0] + 2) // 16) * 16, channels), F32),
+            pltpu.VMEM((row_count, padded, channels), F32),
+            pltpu.VMEM((row_count, key_count, channels), F32),
+            pltpu.SemaphoreType.DMA((CYCLES, ring)),
+            pltpu.SemaphoreType.DMA((CYCLES, ring)),
+            pltpu.SemaphoreType.DMA((len(FETCHED),)),
+        ],
+        compiler_params=pltpu.CompilerParams(collective_id=0, has_side_effects=True),
+        name="cycles",
+    )(
+        res_mask,
+        chain_ids,
+        point_scale,
+        single_in,
+        frames_in.T,
+        dist_bins,
+        res_mask,
+        chain_ids,
+        w_left,
+        w_right,
+        dist_embed,
+        chain_embed,
+        pair_gain,
+        mlp_bias,
+        bias_weight.T,
+        single_gain,
+        w_frame.T,
+        heads,
+        key_slots,
+        shift,
+        pick,
+        *fetched,
+    )
+    return pair, single, frames.T
+
+
 def solution(mesh):
     in_specs = (
         P(("groups", "rows"), "cols", None),
@@ -337,4 +792,7 @@
         P(("groups", "rows"), None),
         P(None, ("groups", "rows")),
     )
-    return jax.shard_map(shards, mesh=mesh, in_specs=in_specs, out_specs=out_specs, check_vma=False)
+    body = shards
+    if mesh.shape["cols"] == 1 and mesh.shape["rows"] > 1:
+        body = functools.partial(dense_shards, mesh.shape["rows"])
+    return jax.shard_map(body, mesh=mesh, in_specs=in_specs, out_specs=out_specs, check_vma=False)

time: 197 us -> 34.7 us (0.18); the launches traced: 195 us -> 34.4 us
  blocking collectives: 115 us -> 0 us
  matrix products: 35.8 us -> 0 us
  Pallas kernels: 0 us -> 29.5 us
  local copies, waits for them, and re-layouts: 30 us -> 4.25 us
  other arithmetic: 11.5 us -> 0 us
    all_gather x6 -> x0, blocking collectives: 115 us -> none  [the longest x2 40.7 us: shards(): lax.all_gather(own_right, 'rows', axis=0, tiled=True)]
    dot_general x60 -> x0, matrix products: 35.2 us -> none  [the longest x16 15.4 us: update_row(): mixed_out = jnp.dot(hidden, mlp_out, preferred_element_type=jnp.float32)]
    pallas_call x0 -> x1, Pallas kernels: none -> 29.5 us  [dense_shards(): pl.pallas_call(functools.partial(cycles_kernel, ring, (head_count, head_d...]
    convert_element_type x22 -> x0, other arithmetic: 8.24 us -> none  [the longest x16 5.94 us: update_row(): chain_embed[1].astype(jnp.float32)]
    dynamic_slice x17 -> x0, local copies, waits for them, and re-layouts: 7.75 us -> none  [the longest x16 7.02 us: shards(): lax.map(row_step, (pair_tile, dist_bins[cycle_index], left_proj, pair_mas...]
    eq x16 -> x0, local copies, waits for them, and re-layouts: 5.66 us -> none  [update_row(): bins_row[:, None]]
    mul x16 -> x0, local copies, waits for them, and re-layouts: 5.61 us -> none  [update_row(): mask_row[:, None] * (left_row[None, :] + right_keys.astype(jnp.float32))]
    reshape x25 -> x0, local copies, waits for them, and re-layouts: 3.41 us -> none  [the longest x3 0.81 us: to_global(): turns = frames[:, :9].reshape(-1, 3, 3)]
where the time goes in v2:
time: 34.7 us; the launch traced here: 34.4 us
  Pallas kernels  29.5 us (85%)
  local copies, waits for them, and re-layouts  4.25 us (12%)
  between operations  0.65 us (2%)
    pallas_call x1, Pallas kernels, dense_shards(): pl.pallas_call(functools.partial(cycles_kernel, ring, (head_count, head_d...  29.5 us
    unnamed x3, local copies, waits for them, and re-layouts  4.25 us

profile of v2, /device:TPU:0, one launch (start us, length us, event | category | flops | bytes accessed | tf_op | source)
XLA Modules:
  0.0 34.4 jit_solution(2412781979798992014)
XLA Ops:
  0.6 29.5 %cycles.1 = (bf16[8,128,128]{2,1,0:T(8,128)(2,1)}, f32[8,384]{1,0:T(8,128)}, f32[8,12]{1,0:T(8,128)}) custom-call(s32[128]{0:T(128)} %refs_6_.1, s32[128]{0:T(128)} %refs_7_.1, f32[12]{0:T(128)} %refs_2_.1, f32[8,384]{1,0:T(8,128)} %refs_3_.1, f32[8,12]{1,0:T(8,128)} %bitcast.9, s32[2,8,128]{2,1,0:T(8,128)} %refs_5_.1, s32[128]{0:T(128)} %refs_6_.1, ...), custom_call_target="tpu_custom_call" | custom-call | tf_op jit(solution)/shard_map/cycles/pallas_call | solution.py:717
  30.2 1.7 %copy.31 = bf16[8,128,128]{2,1,0:T(8,128)(2,1)} copy(bf16[8,128,128]{2,1,0:T(8,128)(2,1)} %get-tuple-element.12) | data formatting | bytes 524288
  31.8 1.3 %copy.32 = f32[8,384]{1,0:T(8,128)} copy(f32[8,384]{1,0:T(8,128)} %get-tuple-element.13) | data formatting | bytes 24576
  33.1 1.3 %copy.33 = f32[12,8]{0,1:T(8,128)} copy(f32[12,8]{0,1:T(8,128)} %bitcast.11) | data formatting | bytes 768

commit v3 on v2

--- a/solution.py
+++ b/solution.py
@@ -426,7 +426,7 @@
 
     def send(cycle):
         copies = []
-        for step in range(1, ring):
+        for step in sorted(range(1, ring), key=lambda step: abs(2 * step - ring)):
             copy = pltpu.make_async_remote_copy(
                 src_ref=s["send"].at[cycle],
                 dst_ref=s["held"].at[cycle, me],
@@ -625,6 +625,28 @@
             copies = send(cycle + 1)
     single_out[...] = single
     frames_out[...] = frames[:, : frames_out.shape[1]]
+
+
+def hand_on_kernel(*refs):
+    count = (len(refs) - 1) // 2
+    copies = [
+        pltpu.make_async_copy(refs[k], refs[count + k], refs[-1].at[k]) for k in range(count)
+    ]
+    for copy in copies:
+        copy.start()
+    for copy in copies:
+        copy.wait()
+
+
+def hand_on(*arrays):
+    return pl.pallas_call(
+        hand_on_kernel,
+        out_shape=tuple(jax.ShapeDtypeStruct(item.shape, item.dtype) for item in arrays),
+        in_specs=[pl.BlockSpec(memory_space=pl.ANY)] * len(arrays),
+        out_specs=(pl.BlockSpec(memory_space=pltpu.VMEM),) * len(arrays),
+        scratch_shapes=[pltpu.SemaphoreType.DMA((len(arrays),))],
+        name="hand_on",
+    )(*arrays)
 
 
 def next_frames(frames, step):
@@ -760,6 +782,7 @@
         pick,
         *fetched,
     )
+    pair, single, frames = hand_on(pair, single, frames)
     return pair, single, frames.T
 
 

time: 34.7 us -> 33.2 us (0.957)
  local copies, waits for them, and re-layouts: 4.25 us -> 0 us
  Pallas kernels: 29.5 us -> 32.4 us
    unnamed x3 -> x0, local copies, waits for them, and re-layouts: 4.25 us -> none
    pallas_call x0 -> x1, Pallas kernels: none -> 1.69 us  [hand_on(): pl.pallas_call(hand_on_kernel, out_shape=tuple((jax.ShapeDtypeStruct(item...]
    pallas_call x1, Pallas kernels: 29.5 us -> 30.7 us  [dense_shards(): pl.pallas_call(functools.partial(cycles_kernel, ring, (head_count, head_d...]
where the time goes in v3:
time: 33.2 us; the launch traced here: 33.1 us
  Pallas kernels  32.4 us (98%)
  between operations  0.65 us (2%)
    pallas_call x1, Pallas kernels, dense_shards(): pl.pallas_call(functools.partial(cycles_kernel, ring, (head_count, head_d...  30.7 us
    pallas_call x1, Pallas kernels, hand_on(): pl.pallas_call(hand_on_kernel, out_shape=tuple((jax.ShapeDtypeStruct(item...  1.69 us

profile of v3, /device:TPU:0, one launch (start us, length us, event | category | flops | bytes accessed | tf_op | source)
XLA Modules:
  0.0 33.1 jit_solution(4652471988640388988)
XLA Ops:
  0.6 30.7 %cycles.1 = (bf16[8,128,128]{2,1,0:T(8,128)(2,1)}, f32[8,384]{1,0:T(8,128)}, f32[8,12]{1,0:T(8,128)}) custom-call(s32[128]{0:T(128)} %refs_6_.1, s32[128]{0:T(128)} %refs_7_.1, f32[12]{0:T(128)} %refs_2_.1, f32[8,384]{1,0:T(8,128)} %refs_3_.1, f32[8,12]{1,0:T(8,128)} %bitcast.9, s32[2,8,128]{2,1,0:T(8,128)} %refs_5_.1, s32[128]{0:T(128)} %refs_6_.1, ...), custom_call_target="tpu_custom_call" | custom-call | tf_op jit(solution)/shard_map/cycles/pallas_call | solution.py:739
  31.4 1.7 %hand_on.1 = (bf16[8,128,128]{2,1,0:T(8,128)(2,1)}, f32[8,384]{1,0:T(8,128)}, f32[8,12]{1,0:T(8,128)}) custom-call(bf16[8,128,128]{2,1,0:T(8,128)(2,1)} %get-tuple-element.9.refs_0_, f32[8,384]{1,0:T(8,128)} %get-tuple-element.10.refs_1_, f32[8,12]{1,0:T(8,128)} %get-tuple-element.11.refs_2_), custom_call_target="tpu_custom_call" | custom-call | tf_op jit(solution)/shard_map/hand_on/pallas_call | solution.py:642

commit v4 on v3

--- a/solution.py
+++ b/solution.py
@@ -363,6 +363,7 @@
     ).astype(F32)
 
 
+PLANE = 4
 IN_PLACE = (
     "mask_smem",
     "chain_smem",
@@ -393,10 +394,15 @@
     "table",
     "sums",
     "base",
+    "live",
     "send_sems",
     "recv_sems",
     "fetch_sems",
 )
+
+
+def plane_order(count):
+    return sorted(range(count), key=lambda far: (min(far, count - far), far))
 
 
 def cycles_kernel(ring, sizes, *refs):
@@ -424,19 +430,31 @@
         fetches[name] = pltpu.make_async_copy(r[name], s[name], s["fetch_sems"].at[k])
         fetches[name].start()
 
+    plane_size = math.gcd(ring, PLANE)
+    plane_count = ring // plane_size
+    plane_rows = plane_size * row_count
+    plane, place = me // plane_size, lax.rem(me, plane_size)
+
     def send(cycle):
-        copies = []
-        for step in sorted(range(1, ring), key=lambda step: abs(2 * step - ring)):
-            copy = pltpu.make_async_remote_copy(
-                src_ref=s["send"].at[cycle],
-                dst_ref=s["held"].at[cycle, me],
-                send_sem=s["send_sems"].at[cycle, step],
-                recv_sem=s["recv_sems"].at[cycle, step],
-                device_id={"rows": lax.rem(me + step, ring)},
-                device_id_type=MESH_ID,
-            )
-            copy.start()
-            copies.append(copy)
+        copies = [[] for _ in range(plane_count)]
+        for far in plane_order(plane_count):
+            for step in range(plane_size):
+                if far == 0 and step == 0:
+                    continue
+                peer = lax.rem(plane + far, plane_count) * plane_size + lax.rem(
+                    place + step, plane_size
+                )
+                slot = far * plane_size + step
+                copy = pltpu.make_async_remote_copy(
+                    src_ref=s["send"].at[cycle],
+                    dst_ref=s["held"].at[cycle, me],
+                    send_sem=s["send_sems"].at[cycle, slot],
+                    recv_sem=s["recv_sems"].at[cycle, slot],
+                    device_id={"rows": peer},
+                    device_id_type=MESH_ID,
+                )
+                copy.start()
+                copies[far].append(copy)
         s["held"][cycle, me] = s["send"][cycle]
         return copies
 
@@ -456,6 +474,7 @@
         (lax.broadcasted_iota(jnp.int32, (16, key_count), 0) == 0) & key_live, 1.0, 0.0
     ).astype(BF16)
     live_column = tn(live_rows, jnp.ones((16, channels), BF16))
+    s["live"][...] = live_column
     gain = r["pair_gain"][...].reshape(1, channels)
     mlp_bias = r["mlp_bias"][...].reshape(1, -1)
     single_gain = r["single_gain"][...].reshape(1, width)
@@ -478,8 +497,10 @@
         scale = jnp.where(head_rows == h, r["scale_smem"][h] * point_weight, scale)
     scale = jnp.concatenate([scale] * row_count, axis=0)
 
+    live_row = [r["mask_smem"][me * row_count + i].astype(F32) for i in range(row_count)]
+
     def mask_of(i):
-        return live_column * r["mask_smem"][me * row_count + i].astype(F32)
+        return live_column * live_row[i]
 
     def spread_heads(values, mask):
         return jnp.concatenate([values[i : i + 1, :] * mask for i in range(row_count)], axis=0)
@@ -537,24 +558,32 @@
             fetches["mlp_in"].wait()
             fetches["mlp_out"].wait()
             fetches["w_out"].wait()
-        for copy in copies:
-            copy.wait()
+        for far in plane_order(plane_count):
+            for copy in copies[far]:
+                copy.wait_recv()
+            source = lax.rem(plane + plane_count - far, plane_count)
+            here = pl.ds(pl.multiple_of(source * plane_rows, plane_rows), plane_rows)
+            arrived = s["held"][cycle, pl.ds(source * plane_size, plane_size)].astype(F32)
+            arrived = arrived.reshape(plane_rows, width + 128)[:, :width].astype(BF16)
+            right = nn(arrived, r["w_right"][...]).astype(BF16).astype(F32)
+            live = s["live"][here, :]
+            masks = jnp.concatenate([live * live_row[i] for i in range(row_count)], axis=0)
+            base = s["base"][:, here, :].reshape(row_count * plane_rows, channels)
+            summed = base + masks * jnp.concatenate([right] * row_count, axis=0)
+            normed = layer_norm(summed, gain).astype(BF16)
+            hidden = jnp.maximum(nn(normed, s["mlp_in"][...]) + mlp_bias, 0.0).astype(BF16)
+            new_pair = (summed + masks * nn(hidden, s["mlp_out"][...])).astype(BF16)
+            pair_out[:, here, :] = new_pair.reshape(row_count, plane_rows, channels)
+        for far in range(plane_count):
+            for copy in copies[far]:
+                copy.wait_send()
+        biases = jnp.concatenate(
+            [nt(bias_rows, pair_out[i]) for i in range(row_count)], axis=0
+        )
 
         everyone = s["held"][cycle].astype(F32).reshape(key_count, width + 128)
         all_single = everyone[:, :width].astype(BF16)
         key_frames = unpack_frames(everyone[:, width:])
-        right = nn(all_single, r["w_right"][...]).astype(BF16).astype(F32)
-        biases = []
-        for i in range(row_count):
-            mask_i = mask_of(i)
-            summed = s["base"][i] + mask_i * right
-            normed = layer_norm(summed, gain).astype(BF16)
-            hidden = jnp.maximum(nn(normed, s["mlp_in"][...]) + mlp_bias, 0.0).astype(BF16)
-            new_pair = (summed + mask_i * nn(hidden, s["mlp_out"][...])).astype(BF16)
-            pair_out[i] = new_pair
-            biases.append(nt(bias_rows, new_pair))
-        biases = jnp.concatenate(biases, axis=0)
-
         keys = nt(all_single, s["w_qkv"][part : 2 * part, :]).astype(BF16)
         values = nt(all_single, s["w_qkv"][2 * part : 3 * part, :]).astype(BF16)
         scores = nt(spread_queries, keys)
@@ -752,6 +781,7 @@
             pltpu.VMEM((-(-(dist_embed.shape[0] + 2) // 16) * 16, channels), F32),
             pltpu.VMEM((row_count, padded, channels), F32),
             pltpu.VMEM((row_count, key_count, channels), F32),
+            pltpu.VMEM((key_count, channels), F32),
             pltpu.SemaphoreType.DMA((CYCLES, ring)),
             pltpu.SemaphoreType.DMA((CYCLES, ring)),
             pltpu.SemaphoreType.DMA((len(FETCHED),)),

time: 33.2 us -> 30.3 us (0.913)
  Pallas kernels: 32.4 us -> 29.5 us
    pallas_call x1, Pallas kernels: 30.7 us -> 27.8 us  [dense_shards(): pl.pallas_call(functools.partial(cycles_kernel, ring, (head_count, head_d...]
where the time goes in v4:
time: 30.3 us; the launch traced here: 30.1 us
  Pallas kernels  29.5 us (97%)
  between operations  0.65 us (2%)
    pallas_call x1, Pallas kernels, dense_shards(): pl.pallas_call(functools.partial(cycles_kernel, ring, (head_count, head_d...  27.8 us
    pallas_call x1, Pallas kernels, hand_on(): pl.pallas_call(hand_on_kernel, out_shape=tuple((jax.ShapeDtypeStruct(item...  1.69 us

profile of v4, /device:TPU:0, one launch (start us, length us, event | category | flops | bytes accessed | tf_op | source)
XLA Modules:
  0.0 30.1 jit_solution(4665754313995503917)
XLA Ops:
  0.6 27.8 %cycles.1 = (bf16[8,128,128]{2,1,0:T(8,128)(2,1)}, f32[8,384]{1,0:T(8,128)}, f32[8,12]{1,0:T(8,128)}) custom-call(s32[128]{0:T(128)} %refs_6_.1, s32[128]{0:T(128)} %refs_7_.1, f32[12]{0:T(128)} %refs_2_.1, f32[8,384]{1,0:T(8,128)} %refs_3_.1, f32[8,12]{1,0:T(8,128)} %bitcast.9, s32[2,8,128]{2,1,0:T(8,128)} %refs_5_.1, s32[128]{0:T(128)} %refs_6_.1, ...), custom_call_target="tpu_custom_call" | custom-call | tf_op jit(solution)/shard_map/cycles/pallas_call | solution.py:768
  28.5 1.7 %hand_on.1 = (bf16[8,128,128]{2,1,0:T(8,128)(2,1)}, f32[8,384]{1,0:T(8,128)}, f32[8,12]{1,0:T(8,128)}) custom-call(bf16[8,128,128]{2,1,0:T(8,128)(2,1)} %get-tuple-element.9.refs_0_, f32[8,384]{1,0:T(8,128)} %get-tuple-element.10.refs_1_, f32[8,12]{1,0:T(8,128)} %get-tuple-element.11.refs_2_), custom_call_target="tpu_custom_call" | custom-call | tf_op jit(solution)/shard_map/hand_on/pallas_call | solution.py:671
